TPU v7x, 32 devices: a whole 2x2x4 slice. The times are simulated.
32 devices in a mesh: gx: 4 (over z), gy: 2 (over x), gz: 4 (over y, core).
Axes of the slice: x: 2, y: 2, z: 4, core: 2. Of those that a mesh axis runs over, the one named last changes fastest.
Arguments:
- volume: bfloat16 [64, 256, 512], P('gz', 'gy', 'gx'), may hold values from 0 to 1
- hat_center: int32 [256], replicated, may hold values from 0 to 255
- tf_table: bfloat16 [4, 256], replicated, may hold values from 0.049804688 to 1
Outputs:
- image: float32 [4, 256, 512], P(None, 'gy')
All inputs are finite; a program needn't handle non-finite values.
Results may differ from a plain program's by a relative error of at most 0.0003.
Values may be sent and summed in bfloat16 or wider, within the bound.
A program may use at most 64 MiB of HBM per device.

v0:
```python
import functools

import jax
import jax.numpy as jnp
from jax import lax
from jax.experimental import pallas as pl
from jax.experimental.pallas import tpu as pltpu
from jax.sharding import PartitionSpec as P

NBIN = 256
HW = 4

ambient = 0.3
grad_floor = 0.01
depth_scale = 1.5

LANES = 128
GROUPS = 7
MESH = pl.DeviceIdType.MESH
F32 = jnp.float32
BF16 = jnp.bfloat16


def build_tables(center_ref, table_ref, tab):
    centers = center_ref[...].astype(F32)
    wide = table_ref[...].astype(F32)
    copies = jnp.concatenate(
        [jnp.broadcast_to(wide[c : c + 1], (8, NBIN)) for c in range(4)], axis=0
    ).astype(BF16)
    centers = jnp.broadcast_to(centers, (LANES, NBIN))
    row = lax.broadcasted_iota(jnp.int32, (LANES, NBIN), 0).astype(F32)
    away = centers - row

    def hats(level):
        return jnp.maximum(0.0, 1.0 - jnp.abs(level - centers) / HW)

    groups = [
        hats((row + LANES) * (1.0 / (2 * LANES)) * (NBIN - 1)),
        jnp.where(away == -3.0, 0.0, jnp.maximum(0.0, 1.0 - jnp.abs(away) / HW)),
        jnp.where((away == 1.0) | (away == 2.0), 1.0, jnp.where((away == 0.0) | (away == -1.0), -1.0, 0.0)),
        jnp.where(away == 3.0, 1.0, jnp.where(away == -2.0, -1.0, 0.0)),
        jnp.where(away == 4.0, 1.0, 0.0),
        jnp.where(away == -3.0, 1.0, 0.0),
        hats(jnp.full((LANES, NBIN), float(NBIN - 1), F32)),
    ]
    for group, weights in enumerate(groups):
        tab[:, group * LANES : (group + 1) * LANES] = lax.dot_general(
            copies, weights.astype(BF16), (((1,), (1,)), ((), ())), preferred_element_type=F32
        )


def lookup(values, tab):
    level = values * float(NBIN - 1)
    bin_index = level.astype(jnp.int32)
    part_bin = level - bin_index.astype(F32)
    quarter = part_bin * 0.25
    coarse = (quarter + 1.5 * 2.0**15) - 1.5 * 2.0**15
    fine = (quarter + 1.5 * 2.0**14) - 1.5 * 2.0**14
    rising = quarter.astype(BF16).astype(F32)
    falling = ((1.0 - part_bin) * 0.25).astype(BF16).astype(F32)
    low_index = bin_index & (LANES - 1)
    high_index = (values * float(2 * LANES)).astype(jnp.int32) & (LANES - 1)
    upper, top = values >= 0.5, values >= 1.0

    def entry(c, group):
        return tab[8 * c : 8 * c + 8, group * LANES : (group + 1) * LANES]

    out = []
    for c in range(4):
        flat, per_coarse, per_fine, per_rising, per_falling = (
            jnp.take_along_axis(entry(c, 1 + k), low_index, axis=1) for k in range(5)
        )
        total = (flat + coarse * per_coarse) + (fine * per_fine + rising * per_rising + falling * per_falling)
        out.append(total)
    for c in range(4):
        high = jnp.take_along_axis(entry(c, 0), high_index, axis=1)
        out[c] = jnp.where(top, entry(c, 6), jnp.where(upper, high, out[c]))
    return out


def body(sizes, vol, center_ref, table_ref, out, tab, xsd, look_a, look_b, look_c, zhalo, face, faces, rows_out, rows_in, part, recv1, recv2, pair,
         zs, zr, fs, fr, rs, rr, es, er, us, ur, ds, dr, ys, yr, cs, cr, qs, qr):
    nx, ny, nz = sizes
    planes, height, across = vol.shape
    ix, iy, iz = lax.axis_index("gx"), lax.axis_index("gy"), lax.axis_index("gz")
    depth = planes * nz

    def at(x, y, z):
        return (x, y, z)

    relations = []
    for s in (-1, 1):
        relations.append((((ix + s >= 0) & (ix + s < nx)), (ix + s, iy, iz)))
        relations.append((((iz + s >= 0) & (iz + s < nz)), (ix, iy, iz + s)))
    for s in (-1, 1):
        for t in (-1, 0, 1):
            relations.append(
                ((iy + s >= 0) & (iy + s < ny) & (ix + t >= 0) & (ix + t < nx), (ix + t, iy + s, iz))
            )
    bit0, bit1 = iz % 2, iz // 2
    near = iz + 1 - 2 * bit0
    far = iz + 2 - 4 * bit1
    faces[...] = jnp.zeros_like(faces)
    rows_in[...] = jnp.zeros_like(rows_in)
    barrier = pltpu.get_barrier_semaphore()
    count = 2
    for there, where in relations:
        count = count + there.astype(jnp.int32)

        @pl.when(there)
        def _(where=where):
            pl.semaphore_signal(barrier, inc=1, device_id=where, device_id_type=MESH)

    for where in ((ix, iy, near), (ix, iy, far)):
        pl.semaphore_signal(barrier, inc=1, device_id=where, device_id_type=MESH)
    pl.semaphore_wait(barrier, count)

    def remote(src, dst, ssem, rsem, where):
        return pltpu.make_async_remote_copy(
            src_ref=src, dst_ref=dst, send_sem=ssem, recv_sem=rsem, device_id=where, device_id_type=MESH
        )

    front, back = iz > 0, iz < nz - 1
    to_back = remote(vol.at[planes - 1], zhalo.at[0], zs.at[0], zr.at[0], (ix, iy, iz + 1))
    to_front = remote(vol.at[0], zhalo.at[1], zs.at[1], zr.at[1], (ix, iy, iz - 1))

    @pl.when(back)
    def _():
        to_back.start()

    @pl.when(front)
    def _():
        to_front.start()

    build_tables(center_ref, table_ref, tab)

    source = lax.broadcasted_iota(jnp.int32, (across, across), 0)
    target = lax.broadcasted_iota(jnp.int32, (across, across), 1)
    gap = source - target
    blur = jnp.where(gap == 0, 2.0, jnp.where(jnp.abs(gap) == 1, 1.0, 0.0))
    slope = jnp.where(gap == 1, 1.0, jnp.where(gap == -1, -1.0, 0.0))
    stencil = jnp.concatenate([blur, slope], axis=1).astype(BF16)

    def edge_columns(cells, plane):
        right = jnp.where((source == across - 1) & (target == 2 * plane + 1), 1.0, 0.0)
        left = jnp.where((source == 0) & (target == 2 * plane), 1.0, 0.0)
        return jnp.dot(cells, (right + left).astype(BF16), preferred_element_type=F32)

    def own_plane(z, acc):
        cells = vol[z]
        xsd[z + 1, pl.ds(8, height), :] = jnp.dot(cells, stencil, preferred_element_type=F32)
        return acc + edge_columns(cells, z + 1)

    columns = lax.fori_loop(0, planes, own_plane, jnp.zeros((height, across), F32))

    @pl.when(back)
    def _():
        to_back.wait_send()
        to_front.wait_recv()

    @pl.when(front)
    def _():
        to_front.wait_send()
        to_back.wait_recv()

    @pl.when(jnp.logical_not(front))
    def _():
        zhalo[0] = jnp.zeros_like(zhalo[0])

    @pl.when(jnp.logical_not(back))
    def _():
        zhalo[1] = jnp.zeros_like(zhalo[1])

    for slot, plane in ((0, 0), (1, planes + 1)):
        cells = zhalo[slot]
        xsd[plane, pl.ds(8, height), :] = jnp.dot(cells, stencil, preferred_element_type=F32)
        columns = columns + edge_columns(cells, plane)
    face[...] = columns.astype(BF16)

    def edge_rows(row):
        own = vol[:, row, :].astype(F32)
        pad = jnp.zeros((rows_out.shape[1] - planes - 2, across), F32)
        ends = [zhalo[slot, row : row + 1, :].astype(F32) for slot in (0, 1)]
        return jnp.concatenate([ends[0], own, ends[1], pad], axis=0).astype(BF16)

    rows_out[0] = edge_rows(0)
    rows_out[1] = edge_rows(height - 1)

    halo = []
    for s, slot in ((1, 0), (-1, 1)):
        sending = (ix + s >= 0) & (ix + s < nx)
        taking = (ix - s >= 0) & (ix - s < nx)
        halo.append((sending, taking, remote(face, faces.at[slot], fs.at[slot], fr.at[slot], (ix + s, iy, iz))))
    for s, side in ((1, 0), (-1, 1)):
        for t in (-1, 0, 1):
            slot = 1 - t
            sending = (iy + s >= 0) & (iy + s < ny) & (ix + t >= 0) & (ix + t < nx)
            taking = (iy - s >= 0) & (iy - s < ny) & (ix - t >= 0) & (ix - t < nx)
            halo.append(
                (sending, taking, remote(rows_out.at[1 - side], rows_in.at[side, slot], rs.at[side, slot], rr.at[side, slot], (ix + t, iy + s, iz)))
            )
    for sending, _, copy in halo:

        @pl.when(sending)
        def _(copy=copy):
            copy.start()

    half, band = height // 2, height // 4
    keep, give = bit0 * half, (1 - bit0) * half
    keep2, give2 = bit1 * band, (1 - bit1) * band

    def look_rows(table, z, start, count):
        cells = vol[z, pl.ds(pl.multiple_of(start, 16), count), :].astype(F32)
        for k in range(count // 8):
            four = lookup(cells[8 * k : 8 * k + 8], tab)
            for c in range(4):
                table[c, z, 8 * k : 8 * k + 8, :] = four[c]

    def look_give(z, carry):
        look_rows(look_a, z, give, half)
        return carry

    lax.fori_loop(0, planes, look_give, 0)

    for sending, taking, copy in halo:

        @pl.when(taking)
        def _(copy=copy):
            copy.wait_recv()

        @pl.when(sending)
        def _(copy=copy):
            copy.wait_send()

    lane = lax.broadcasted_iota(jnp.int32, (height, across), 1)
    both = jnp.where(lane % 2 == 1, faces[0].astype(F32), faces[1].astype(F32))
    ends = jnp.where((lane == 0) | (lane == across - 1), 1.0, 0.0)
    sign = jnp.where(lane == 0, -1.0, jnp.where(lane == across - 1, 1.0, 0.0))

    def add_columns(z, carry):
        placed = pltpu.roll(both, across - 2 * z - 1, 1)
        xsd[z, pl.ds(8, height), :] += jnp.concatenate([placed * ends, placed * sign], axis=1)
        return carry

    lax.fori_loop(0, planes + 2, add_columns, 0)
    count_rows = rows_out.shape[1]
    for side in (0, 1):
        strip = jnp.dot(rows_in[side, 1], stencil, preferred_element_type=F32)
        left = pltpu.roll(rows_in[side, 0].astype(F32), 1, 1)
        right = pltpu.roll(rows_in[side, 2].astype(F32), across - 1, 1)
        short = lax.broadcasted_iota(jnp.int32, (count_rows, across), 1)
        left = jnp.where(short == 0, left, 0.0)
        right = jnp.where(short == across - 1, right, 0.0)
        strip = strip + jnp.concatenate([left + right, right - left], axis=1)
        row = 7 if side == 0 else 8 + height
        for z in range(planes + 2):
            xsd[z, row : row + 1, :] = strip[z : z + 1]

    shade_scale = (1.0 - ambient) / (32.0 * 3.0**0.5)

    sub = lax.broadcasted_iota(jnp.int32, (8, 2 * across), 0)

    def march(row, table, own):
        def gradients(z):
            above = xsd[z, pl.ds(row, 8), :]
            mid = xsd[z, pl.ds(row + 8, 8), :]
            below = xsd[z, pl.ds(row + 16, 8), :]
            up = pltpu.roll(jnp.where(sub == 7, above, mid), 1, 0)
            down = pltpu.roll(jnp.where(sub == 0, below, mid), 7, 0)
            smoothed = up + 2.0 * mid + down
            return smoothed[:, across:], down[:, :across] - up[:, :across], smoothed[:, :across]

        through = jnp.ones((8, across), F32)
        sums = [jnp.zeros((8, across), F32) for _ in range(3)]
        before, here = gradients(0), gradients(1)
        for z in range(planes):
            after = gradients(z + 2)
            grad_x = before[0] + 2.0 * here[0] + after[0]
            grad_y = before[1] + 2.0 * here[1] + after[1]
            grad_z = after[2] - before[2]
            before, here = here, after
            square = (grad_x * grad_x + grad_y * grad_y + grad_z * grad_z) * (1.0 / 1024.0) + grad_floor
            shade = ambient + shade_scale * jnp.abs(grad_x + grad_y + grad_z) * lax.rsqrt(square)
            clear = jnp.exp(table[3, z, pl.ds(own, 8), :] * (-depth_scale / depth))
            weight = through * (1.0 - clear) * shade
            for c in range(3):
                sums[c] = sums[c] + weight * table[c, z, pl.ds(own, 8), :]
            through = through * clear
        for c in range(3):
            part[c, pl.ds(row, 8), :] = sums[c]
        part[3, pl.ds(row, 8), :] = through

    def march_rows(start, table, count, along=None):
        def step(n, carry):
            march(pl.multiple_of(start + 8 * n, 8), table, pl.multiple_of(8 * n, 8))
            if along is not None:
                along(n)
            return carry

        lax.fori_loop(0, count // 8, step, 0)

    share = planes // (half // 8)

    def look_give2(n):
        for k in range(share):
            look_rows(look_b, share * n + k, keep + give2, band)

    march_rows(give, look_a, half, look_give2)
    first = remote(part.at[:, pl.ds(pl.multiple_of(give, half), half), :], recv1, es.at[0], er.at[0], (ix, iy, near))
    first.start()
    march_rows(keep + give2, look_b, band)
    first.wait_recv()

    def fold(mine, theirs, i_am_front):
        ahead = jnp.where(i_am_front, mine[3], theirs[3])
        mixed = []
        for c in range(3):
            a = jnp.where(i_am_front, mine[c], theirs[c])
            b = jnp.where(i_am_front, theirs[c], mine[c])
            mixed.append(a + ahead * b)
        mixed.append(mine[3] * theirs[3])
        return mixed

    def pair_of(start):
        own = pl.ds(pl.multiple_of(keep + start, band), band)
        other = pl.ds(pl.multiple_of(start, band), band)
        return fold([part[c, own, :] for c in range(4)], [recv1[c, other, :] for c in range(4)], bit0 == 0)

    for c, value in enumerate(pair_of(give2)):
        pair[c] = value
    second = remote(pair, recv2, es.at[1], er.at[1], (ix, iy, far))
    second.start()

    def look_keep2(n, carry):
        for k in range(2):
            look_rows(look_c, 2 * n + k, keep + keep2, band)
        return carry

    lax.fori_loop(0, planes // 2, look_keep2, 0)
    march_rows(keep + keep2, look_c, band)
    mine = pair_of(keep2)
    second.wait_recv()
    quad = fold(mine, [recv2[c] for c in range(4)], bit1 == 0)
    quad[3] = 1.0 - quad[3]

    def region(j, z, h):
        b = (z % 2) * 2 + z // 2
        return out.at[2 * h : 2 * h + 2, pl.ds(pl.multiple_of(b * band, band), band), pl.ds(pl.multiple_of(j * across, across), across)]

    for c in range(4):
        region(ix, iz, c // 2)[c % 2] = quad[c]

    def up(j, t, h):
        return remote(region(j, iz, h), region(j, iz, h), us.at[t, h], ur.at[t, h], (ix + 1, iy, iz))

    def down(j, t, h):
        return remote(region(j, iz, h), region(j, iz, h), ds.at[t, h], dr.at[t, h], (ix - 1, iy, iz))

    def over(j, slot, h):
        return remote(region(j, iz, h), region(j, iz, h), ys.at[slot, h], yr.at[slot, h], (ix, iy, far))

    def side(j, slot, h):
        return remote(region(j, iz, h), region(j, iz, h), cs.at[slot, h], cr.at[slot, h], (ix, iy, near))

    def side_far(j, slot, h):
        return remote(region(j, far, h), region(j, far, h), qs.at[slot, h], qr.at[slot, h], (ix, iy, near))

    def take_over(j, slot, h):
        return remote(region(j, far, h), region(j, far, h), ys.at[slot, h], yr.at[slot, h], (ix, iy, far))

    far_near = near + 2 - 4 * bit1

    def spread(j, t, slot, h, upward, downward):
        if upward and t < nx - 1:

            @pl.when(ix + 1 < nx)
            def _():
                up(j, t, h).start()

        if downward and t < nx - 1:

            @pl.when(ix >= 1)
            def _():
                down(j, t, h).start()

        over(j, slot, h).start()
        side(j, slot, h).start()

    def relay(j, slot):
        for h in range(2):
            take_over(j, slot, h).wait_recv()
            side_far(j, slot, h).start()

    for h in range(2):
        spread(ix, 0, 0, h, True, True)
    for t in range(1, nx):
        for h in range(2):

            @pl.when(ix >= t)
            def _(t=t, h=h):
                up(ix - t, t - 1, h).wait_recv()
                spread(ix - t, t, 2 * t - 1, h, True, False)

            @pl.when(ix + t < nx)
            def _(t=t, h=h):
                down(ix + t, t - 1, h).wait_recv()
                spread(ix + t, t, 2 * t, h, False, True)

        if t == 1:
            relay(ix, 0)
        else:

            @pl.when(ix >= t - 1)
            def _(t=t):
                relay(ix - t + 1, 2 * t - 3)

            @pl.when(ix + t - 1 < nx)
            def _(t=t):
                relay(ix + t - 1, 2 * t - 2)

    if nx == 1:
        relay(ix, 0)
    else:

        @pl.when(ix >= nx - 1)
        def _():
            relay(ix - nx + 1, 2 * nx - 3)

        @pl.when(ix + nx - 1 < nx)
        def _():
            relay(ix + nx - 1, 2 * nx - 2)

    def finish(j, slot):
        for h in range(2):
            over(j, slot, h).wait_send()
            side(j, slot, h).wait_send()
            side_far(j, slot, h).wait_send()
            ours, others = region(j, near, h), region(j, far_near, h)
            remote(ours, ours, cs.at[slot, h], cr.at[slot, h], (ix, iy, near)).wait_recv()
            remote(others, others, qs.at[slot, h], qr.at[slot, h], (ix, iy, near)).wait_recv()

    finish(ix, 0)
    for t in range(1, nx):

        @pl.when(ix >= t)
        def _(t=t):
            finish(ix - t, 2 * t - 1)

        @pl.when(ix + t < nx)
        def _(t=t):
            finish(ix + t, 2 * t)

    for t in range(nx - 1):

        @pl.when((ix >= t) & (ix + 1 < nx))
        def _(t=t):
            for h in range(2):
                up(ix - t, t, h).wait_send()

        @pl.when((ix + t < nx) & (ix >= 1))
        def _(t=t):
            for h in range(2):
                down(ix + t, t, h).wait_send()

    first.wait_send()
    second.wait_send()


def shards(volume, hat_center, tf_table):
    planes, height, across = volume.shape
    sizes = tuple(lax.axis_size(a) for a in ("gx", "gy", "gz"))
    nx = sizes[0]
    assert sizes[2] == 4 and across == LANES
    extended_rows = -(-(planes + 2) // 16) * 16
    dma = pltpu.SemaphoreType.DMA
    vmem = pl.BlockSpec(memory_space=pltpu.VMEM)
    return pl.pallas_call(
        functools.partial(body, sizes),
        out_shape=jax.ShapeDtypeStruct((4, height, across * nx), F32),
        in_specs=[vmem] * 3,
        out_specs=vmem,
        scratch_shapes=[
            pltpu.VMEM((32, GROUPS * LANES), F32),
            pltpu.VMEM((planes + 2, height + 16, 2 * across), F32),
            pltpu.VMEM((4, planes, height // 2, across), F32),
            pltpu.VMEM((4, planes, height // 4, across), F32),
            pltpu.VMEM((4, planes, height // 4, across), F32),
            pltpu.VMEM((2, height, across), BF16),
            pltpu.VMEM((height, across), BF16),
            pltpu.VMEM((2, height, across), BF16),
            pltpu.VMEM((2, extended_rows, across), BF16),
            pltpu.VMEM((2, 3, extended_rows, across), BF16),
            pltpu.VMEM((4, height, across), F32),
            pltpu.VMEM((4, height // 2, across), F32),
            pltpu.VMEM((4, height // 4, across), F32),
            pltpu.VMEM((4, height // 4, across), F32),
            dma((2,)), dma((2,)),
            dma((2,)), dma((2,)),
            dma((2, 3)), dma((2, 3)),
            dma((2,)), dma((2,)),
            dma((nx, 2)), dma((nx, 2)),
            dma((nx, 2)), dma((nx, 2)),
            dma((2 * nx, 2)), dma((2 * nx, 2)),
            dma((2 * nx, 2)), dma((2 * nx, 2)),
            dma((2 * nx, 2)), dma((2 * nx, 2)),
        ],
        compiler_params=pltpu.CompilerParams(collective_id=0, has_side_effects=True, vmem_limit_bytes=48 << 20),
    )(volume, hat_center.reshape(1, -1), tf_table)


def solution(mesh):
    in_specs = (P("gz", "gy", "gx"), P(), P())
    out_specs = P(None, "gy", None)
    return jax.shard_map(shards, mesh=mesh, in_specs=in_specs, out_specs=out_specs, check_vma=False)
```

profile of v0, /device:TPU:0, one launch (start us, length us, event | category | flops | bytes accessed | tf_op | source)
XLA Modules:
  0.0 40.9 jit_solution(9210418359668454827)
XLA Ops:
  0.0 0.0 copy-start.2
  0.0 0.7 %copy-done.2 = s32[256]{0:T(256)S(1)} copy-done((s32[256]{0:T(256)S(1)}, s32[256]{0:T(256)}, u32[]{:S(2)}) %copy-start.2) | copy-done | bytes 1048
  0.7 0.0 copy-start
  0.7 1.0 %copy-done = bf16[16,128,128]{2,1,0:T(8,128)(2,1)S(1)} copy-done((bf16[16,128,128]{2,1,0:T(8,128)(2,1)S(1)}, bf16[16,128,128]{2,1,0:T(8,128)(2,1)}, u32[]{:S(2)}) %copy-start) | copy-done | bytes 524312
  1.7 0.0 copy-start.1
  1.7 0.7 %copy-done.1 = bf16[4,256]{1,0:T(4,128)(2,1)S(1)} copy-done((bf16[4,256]{1,0:T(4,128)(2,1)S(1)}, bf16[4,256]{1,0:T(4,128)(2,1)}, u32[]{:S(2)}) %copy-start.1) | copy-done | bytes 2072
  2.4 37.5 %shard_map.37 = f32[4,128,512]{2,1,0:T(8,128)S(1)} custom-call(bf16[16,128,128]{2,1,0:T(8,128)(2,1)S(1)} %copy-done, s32[1,256]{1,0:T(1,128)S(1)} %bitcast.1, bf16[4,256]{1,0:T(4,128)(2,1)S(1)} %copy-done.1), custom_call_target="tpu_custom_call" | custom-call | tf_op jit(solution)/shard_map/pallas_call | solution.py:477
  39.9 1.0 %copy.5 = f32[4,128,512]{2,1,0:T(8,128)} copy(f32[4,128,512]{2,1,0:T(8,128)S(1)} %shard_map.37) | data formatting | bytes 2097152
Async XLA Ops:
  0.0 0.7 %copy-start.2 = (s32[256]{0:T(256)S(1)}, s32[256]{0:T(256)}, u32[]{:S(2)}) copy-start(s32[256]{0:T(256)} %param.4) | copy-start | bytes 3076
  0.7 1.0 %copy-start = (bf16[16,128,128]{2,1,0:T(8,128)(2,1)S(1)}, bf16[16,128,128]{2,1,0:T(8,128)(2,1)}, u32[]{:S(2)}) copy-start(bf16[16,128,128]{2,1,0:T(8,128)(2,1)} %vol.1) | copy-start | bytes 1572868
  1.7 0.7 %copy-start.1 = (bf16[4,256]{1,0:T(4,128)(2,1)S(1)}, bf16[4,256]{1,0:T(4,128)(2,1)}, u32[]{:S(2)}) copy-start(bf16[4,256]{1,0:T(4,128)(2,1)} %table_ref.1) | copy-start | bytes 6148
where the time goes:
time: 41.1 us; the launch traced here: 40.9 us
  Pallas kernels  37.5 us (91%)
  local copies, waits for them, and re-layouts  3.37 us (8%)
    pallas_call x1, Pallas kernels, shards(): pl.pallas_call(functools.partial(body, sizes), out_shape=jax.ShapeDtypeSt...  37.5 us
    unnamed x7, local copies, waits for them, and re-layouts  3.37 us

commit v1 on v0

v1 whole, which is shorter than its diff:
```python
import functools

import jax
import jax.numpy as jnp
from jax import lax
from jax.experimental import pallas as pl
from jax.experimental.pallas import tpu as pltpu
from jax.sharding import PartitionSpec as P

NBIN = 256
HW = 4

ambient = 0.3
grad_floor = 0.01
depth_scale = 1.5

LANES = 128
GROUPS = 7
PHASES = 4
AHEAD = 2
STEPS = 65534.0
FINE = 64.0
MESH = pl.DeviceIdType.MESH
F32 = jnp.float32
I16 = jnp.int16
I32 = jnp.int32
BF16 = jnp.bfloat16


def build_tables(center_ref, table_ref, tab):
    centers = center_ref[...].astype(F32)
    wide = table_ref[...].astype(F32)
    copies = jnp.concatenate(
        [jnp.broadcast_to(wide[c : c + 1], (8, NBIN)) for c in range(4)], axis=0
    ).astype(BF16)
    centers = jnp.broadcast_to(centers, (LANES, NBIN))
    row = lax.broadcasted_iota(jnp.int32, (LANES, NBIN), 0).astype(F32)
    away = centers - row

    def hats(level):
        return jnp.maximum(0.0, 1.0 - jnp.abs(level - centers) / HW)

    groups = [
        hats((row + LANES) * (1.0 / (2 * LANES)) * (NBIN - 1)),
        jnp.where(away == -3.0, 0.0, jnp.maximum(0.0, 1.0 - jnp.abs(away) / HW)),
        jnp.where((away == 1.0) | (away == 2.0), 1.0, jnp.where((away == 0.0) | (away == -1.0), -1.0, 0.0)),
        jnp.where(away == 3.0, 1.0, jnp.where(away == -2.0, -1.0, 0.0)),
        jnp.where(away == 4.0, 1.0, 0.0),
        jnp.where(away == -3.0, 1.0, 0.0),
        hats(jnp.full((LANES, NBIN), float(NBIN - 1), F32)),
    ]
    for group, weights in enumerate(groups):
        tab[:, group * LANES : (group + 1) * LANES] = lax.dot_general(
            copies, weights.astype(BF16), (((1,), (1,)), ((), ())), preferred_element_type=F32
        )


def lookup(values, tab):
    level = values * float(NBIN - 1)
    bin_index = level.astype(jnp.int32)
    part_bin = level - bin_index.astype(F32)
    quarter = part_bin * 0.25
    coarse = (quarter + 1.5 * 2.0**15) - 1.5 * 2.0**15
    fine = (quarter + 1.5 * 2.0**14) - 1.5 * 2.0**14
    rising = quarter.astype(BF16).astype(F32)
    falling = ((1.0 - part_bin) * 0.25).astype(BF16).astype(F32)
    low_index = bin_index & (LANES - 1)
    high_index = (values * float(2 * LANES)).astype(jnp.int32) & (LANES - 1)
    upper, top = values >= 0.5, values >= 1.0

    def entry(c, group):
        return tab[8 * c : 8 * c + 8, group * LANES : (group + 1) * LANES]

    out = []
    for c in range(4):
        flat, per_coarse, per_fine, per_rising, per_falling = (
            jnp.take_along_axis(entry(c, 1 + k), low_index, axis=1) for k in range(5)
        )
        total = (flat + coarse * per_coarse) + (fine * per_fine + rising * per_rising + falling * per_falling)
        out.append(total)
    for c in range(4):
        high = jnp.take_along_axis(entry(c, 0), high_index, axis=1)
        out[c] = jnp.where(top, entry(c, 6), jnp.where(upper, high, out[c]))
    return out


def fold(mine, theirs, i_am_front):
    ahead = jnp.where(i_am_front, mine[3], theirs[3])
    mixed = []
    for c in range(3):
        a = jnp.where(i_am_front, mine[c], theirs[c])
        b = jnp.where(i_am_front, theirs[c], mine[c])
        mixed.append(a + ahead * b)
    mixed.append(mine[3] * theirs[3])
    return mixed


def encode(values, code):
    rows, across = values[0].shape
    row = lax.broadcasted_iota(jnp.int32, (rows, across), 0)
    powers = jnp.zeros((rows, across), I32)
    for c in range(4):
        top = jnp.maximum(jnp.max(values[c], axis=0, keepdims=True), 1e-30)
        power = jnp.floor(jnp.log(top) * (FINE * 1.4426950408889634)) + 2.0
        level = values[c] * (jnp.exp2(power * (-1.0 / FINE)) * STEPS) + 0.5
        code[c] = (jnp.minimum(level, STEPS).astype(I32) - 32767).astype(I16)
        powers = jnp.where(row == c, power.astype(I32), powers)
    code[4] = powers.astype(I16)


def decode(code, c):
    power = code[4].astype(I32).astype(F32)[c : c + 1]
    return (code[c].astype(I32).astype(F32) + 32767.0) * (jnp.exp2(power * (1.0 / FINE)) * (1.0 / STEPS))


def body(sizes, vol_in, center_in, table_in, out, vol, center_ref, table_ref, tab, xsd, look, zhalo, face, faces, rows_out, rows_in, part, recv, code,
         ls, zs, zr, fs, fr, rs, rr, ps, pr, gs, gr, ns, nr):
    nx, ny, nz = sizes
    planes, height, across = vol.shape
    ix, iy, iz = lax.axis_index("gx"), lax.axis_index("gy"), lax.axis_index("gz")
    depth = planes * nz
    bit0, bit1 = iz % 2, iz // 2
    near = iz + 1 - 2 * bit0
    far = iz + 2 - 4 * bit1
    diag = near + 2 - 4 * bit1

    loads = [
        pltpu.make_async_copy(src, dst, ls.at[n])
        for n, (src, dst) in enumerate(((vol_in, vol), (center_in, center_ref), (table_in, table_ref)))
    ]
    for load in loads:
        load.start()

    faces[...] = jnp.zeros_like(faces)
    rows_in[...] = jnp.zeros_like(rows_in)
    barrier = pltpu.get_barrier_semaphore()
    for there in (near, far, diag):
        pl.semaphore_signal(barrier, inc=1, device_id=(ix, iy, there), device_id_type=MESH)
    for t in range(1, nx):
        pl.semaphore_signal(barrier, inc=1, device_id=((ix + t) % nx, iy, iz), device_id_type=MESH)
    count = 2 + nx
    for s in (-1, 1):
        for t in (-1, 0, 1):
            there = (iy + s >= 0) & (iy + s < ny) & (ix + t >= 0) & (ix + t < nx)
            count = count + there.astype(jnp.int32)

            @pl.when(there)
            def _(s=s, t=t):
                pl.semaphore_signal(barrier, inc=1, device_id=(ix + t, iy + s, iz), device_id_type=MESH)

    def remote(src, dst, ssem, rsem, where):
        return pltpu.make_async_remote_copy(
            src_ref=src, dst_ref=dst, send_sem=ssem, recv_sem=rsem, device_id=where, device_id_type=MESH
        )

    front, back = iz > 0, iz < nz - 1
    to_back = remote(vol.at[planes - 1], zhalo.at[0], zs.at[0], zr.at[0], (ix, iy, iz + 1))
    to_front = remote(vol.at[0], zhalo.at[1], zs.at[1], zr.at[1], (ix, iy, iz - 1))

    loads[1].wait()
    loads[2].wait()
    build_tables(center_ref, table_ref, tab)
    loads[0].wait()

    source = lax.broadcasted_iota(jnp.int32, (across, across), 0)
    target = lax.broadcasted_iota(jnp.int32, (across, across), 1)
    gap = source - target
    blur = jnp.where(gap == 0, 2.0, jnp.where(jnp.abs(gap) == 1, 1.0, 0.0))
    slope = jnp.where(gap == 1, 1.0, jnp.where(gap == -1, -1.0, 0.0))
    stencil = jnp.concatenate([blur, slope], axis=1).astype(BF16)

    def edge_columns(cells, plane):
        right = jnp.where((source == across - 1) & (target == 2 * plane + 1), 1.0, 0.0)
        left = jnp.where((source == 0) & (target == 2 * plane), 1.0, 0.0)
        return jnp.dot(cells, (right + left).astype(BF16), preferred_element_type=F32)

    def own_plane(z, acc):
        cells = vol[z]
        xsd[z + 1, pl.ds(8, height), :] = jnp.dot(cells, stencil, preferred_element_type=F32)
        return acc + edge_columns(cells, z + 1)

    pl.semaphore_wait(barrier, count)

    @pl.when(back)
    def _():
        to_back.start()

    @pl.when(front)
    def _():
        to_front.start()

    columns = lax.fori_loop(0, planes, own_plane, jnp.zeros((height, across), F32))

    block = height // (2 * PHASES)

    def start_of(b):
        side = bit0 if b % 2 else 1 - bit0
        return pl.multiple_of((b // 2) * 2 * block + side * block, 16)

    def look_plane(b, z):
        cells = vol[z, pl.ds(start_of(b), block), :].astype(F32)
        for k in range(block // 8):
            four = lookup(cells[8 * k : 8 * k + 8], tab)
            for c in range(4):
                look[b, c, z, 8 * k : 8 * k + 8, :] = four[c]

    def look_block(b):
        def step(n, carry):
            for k in range(4):
                look_plane(b, 4 * n + k)
            return carry

        lax.fori_loop(0, planes // 4, step, 0)

    look_block(0)

    @pl.when(back)
    def _():
        to_back.wait_send()
        to_front.wait_recv()

    @pl.when(front)
    def _():
        to_front.wait_send()
        to_back.wait_recv()

    @pl.when(jnp.logical_not(front))
    def _():
        zhalo[0] = jnp.zeros_like(zhalo[0])

    @pl.when(jnp.logical_not(back))
    def _():
        zhalo[1] = jnp.zeros_like(zhalo[1])

    for slot, plane in ((0, 0), (1, planes + 1)):
        cells = zhalo[slot]
        xsd[plane, pl.ds(8, height), :] = jnp.dot(cells, stencil, preferred_element_type=F32)
        columns = columns + edge_columns(cells, plane)
    face[...] = columns.astype(BF16)

    def edge_rows(row):
        own = vol[:, row, :].astype(F32)
        pad = jnp.zeros((rows_out.shape[1] - planes - 2, across), F32)
        ends = [zhalo[slot, row : row + 1, :].astype(F32) for slot in (0, 1)]
        return jnp.concatenate([ends[0], own, ends[1], pad], axis=0).astype(BF16)

    rows_out[0] = edge_rows(0)
    rows_out[1] = edge_rows(height - 1)

    halo = []
    for s, slot in ((1, 0), (-1, 1)):
        sending = (ix + s >= 0) & (ix + s < nx)
        taking = (ix - s >= 0) & (ix - s < nx)
        halo.append((sending, taking, remote(face, faces.at[slot], fs.at[slot], fr.at[slot], (ix + s, iy, iz))))
    for s, side in ((1, 0), (-1, 1)):
        for t in (-1, 0, 1):
            slot = 1 - t
            sending = (iy + s >= 0) & (iy + s < ny) & (ix + t >= 0) & (ix + t < nx)
            taking = (iy - s >= 0) & (iy - s < ny) & (ix - t >= 0) & (ix - t < nx)
            halo.append(
                (sending, taking, remote(rows_out.at[1 - side], rows_in.at[side, slot], rs.at[side, slot], rr.at[side, slot], (ix + t, iy + s, iz)))
            )
    for sending, _, copy in halo:

        @pl.when(sending)
        def _(copy=copy):
            copy.start()

    for b in range(1, AHEAD):
        look_block(b)

    for sending, taking, copy in halo:

        @pl.when(taking)
        def _(copy=copy):
            copy.wait_recv()

        @pl.when(sending)
        def _(copy=copy):
            copy.wait_send()

    lane = lax.broadcasted_iota(jnp.int32, (height, across), 1)
    both = jnp.where(lane % 2 == 1, faces[0].astype(F32), faces[1].astype(F32))
    ends = jnp.where((lane == 0) | (lane == across - 1), 1.0, 0.0)
    sign = jnp.where(lane == 0, -1.0, jnp.where(lane == across - 1, 1.0, 0.0))

    def add_columns(z, carry):
        placed = pltpu.roll(both, across - 2 * z - 1, 1)
        xsd[z, pl.ds(8, height), :] += jnp.concatenate([placed * ends, placed * sign], axis=1)
        return carry

    lax.fori_loop(0, planes + 2, add_columns, 0)
    count_rows = rows_out.shape[1]
    for side in (0, 1):
        strip = jnp.dot(rows_in[side, 1], stencil, preferred_element_type=F32)
        left = pltpu.roll(rows_in[side, 0].astype(F32), 1, 1)
        right = pltpu.roll(rows_in[side, 2].astype(F32), across - 1, 1)
        short = lax.broadcasted_iota(jnp.int32, (count_rows, across), 1)
        left = jnp.where(short == 0, left, 0.0)
        right = jnp.where(short == across - 1, right, 0.0)
        strip = strip + jnp.concatenate([left + right, right - left], axis=1)
        row = 7 if side == 0 else 8 + height
        for z in range(planes + 2):
            xsd[z, row : row + 1, :] = strip[z : z + 1]

    shade_scale = (1.0 - ambient) / (32.0 * 3.0**0.5)

    sub = lax.broadcasted_iota(jnp.int32, (8, 2 * across), 0)

    def march(b, own):
        row = pl.multiple_of(start_of(b) + own, 8)

        def gradients(z):
            above = xsd[z, pl.ds(row, 8), :]
            mid = xsd[z, pl.ds(row + 8, 8), :]
            below = xsd[z, pl.ds(row + 16, 8), :]
            up = pltpu.roll(jnp.where(sub == 7, above, mid), 1, 0)
            down = pltpu.roll(jnp.where(sub == 0, below, mid), 7, 0)
            smoothed = up + 2.0 * mid + down
            return smoothed[:, across:], down[:, :across] - up[:, :across], smoothed[:, :across]

        through = jnp.ones((8, across), F32)
        sums = [jnp.zeros((8, across), F32) for _ in range(3)]
        before, here = gradients(0), gradients(1)
        for z in range(planes):
            after = gradients(z + 2)
            grad_x = before[0] + 2.0 * here[0] + after[0]
            grad_y = before[1] + 2.0 * here[1] + after[1]
            grad_z = after[2] - before[2]
            before, here = here, after
            square = (grad_x * grad_x + grad_y * grad_y + grad_z * grad_z) * (1.0 / 1024.0) + grad_floor
            shade = ambient + shade_scale * jnp.abs(grad_x + grad_y + grad_z) * lax.rsqrt(square)
            clear = jnp.exp(look[b, 3, z, pl.ds(own, 8), :] * (-depth_scale / depth))
            weight = through * (1.0 - clear) * shade
            for c in range(3):
                sums[c] = sums[c] + weight * look[b, c, z, pl.ds(own, 8), :]
            through = through * clear
        for c in range(3):
            part[b, c, pl.ds(own, 8), :] = sums[c]
        part[b, 3, pl.ds(own, 8), :] = through

    groups = block // 8
    share = planes // groups

    def render(b):
        def step(n, carry):
            march(b, pl.multiple_of(8 * n, 8))
            if b + AHEAD < 2 * PHASES:
                for k in range(share):
                    look_plane(b + AHEAD, share * n + k)
            return carry

        lax.fori_loop(0, groups, step, 0)

    def to_near(p):
        return remote(part.at[2 * p], recv.at[p, 0], ps.at[p, 0], pr.at[p, 0], (ix, iy, near))

    def to_far(p):
        return remote(part.at[2 * p + 1], recv.at[p, 1], ps.at[p, 1], pr.at[p, 1], (ix, iy, far))

    def to_diag(p):
        return remote(part.at[2 * p], recv.at[p, 2], ps.at[p, 2], pr.at[p, 2], (ix, iy, diag))

    def along(p, t):
        tile = code.at[p, bit0, ix]
        return remote(tile, tile, gs.at[p, t - 1], gr.at[p, t - 1], ((ix + t) % nx, iy, iz))

    def hand(p):
        half = code.at[p, bit0]
        return remote(half, half, ns.at[p], nr.at[p], (ix, iy, near))

    def composite(p):
        for copy in (to_near(p), to_diag(p), to_far(p)):
            copy.wait_recv()
        mine = fold([part[2 * p + 1, c] for c in range(4)], [recv[p, 0, c] for c in range(4)], bit0 == 0)
        others = fold([recv[p, 1, c] for c in range(4)], [recv[p, 2, c] for c in range(4)], bit0 == 0)
        quad = fold(mine, others, bit1 == 0)
        quad[3] = 1.0 - quad[3]
        encode(quad, code.at[p, bit0, ix])
        for t in range(nx - 1, 0, -1):
            along(p, t).start()

    def show(p, side):
        rows = pl.ds(pl.multiple_of(p * 2 * block + side * block, 16), block)
        for j in range(nx):
            for c in range(4):
                out[c, rows, j * across : (j + 1) * across] = decode(code.at[p, side, j], c)

    def pass_on(p):
        for t in range(1, nx):
            along(p, t).wait_recv()
        hand(p).start()

    def take(p):
        half = code.at[p, 1 - bit0]
        remote(half, half, ns.at[p], nr.at[p], (ix, iy, near)).wait_recv()
        show(p, 1 - bit0)

    for b in range(2 * PHASES):
        render(b)
        p = b // 2
        if b % 2 == 0:
            to_diag(p).start()
            to_near(p).start()
            if p >= 1:
                composite(p - 1)
        else:
            to_far(p).start()
            if p >= 2:
                pass_on(p - 2)
                show(p - 2, bit0)
    last = PHASES - 1
    for p in range(max(PHASES - 2, 0)):
        take(p)
    composite(last)
    for p in range(max(PHASES - 2, 0), PHASES):
        pass_on(p)
        show(p, bit0)
        take(p)

    for p in range(PHASES):
        for copy in (to_near(p), to_diag(p), to_far(p), hand(p)):
            copy.wait_send()
        for t in range(1, nx):
            along(p, t).wait_send()


def shards(volume, hat_center, tf_table):
    planes, height, across = volume.shape
    sizes = tuple(lax.axis_size(a) for a in ("gx", "gy", "gz"))
    nx = sizes[0]
    assert sizes[2] == 4 and across == LANES and height % (32 * PHASES) == 0
    extended_rows = -(-(planes + 2) // 16) * 16
    block = height // (2 * PHASES)
    dma = pltpu.SemaphoreType.DMA
    vmem = pl.BlockSpec(memory_space=pltpu.VMEM)
    hbm = pl.BlockSpec(memory_space=pltpu.MemorySpace.HBM)
    return pl.pallas_call(
        functools.partial(body, sizes),
        out_shape=jax.ShapeDtypeStruct((4, height, across * nx), F32),
        in_specs=[hbm] * 3,
        out_specs=vmem,
        scratch_shapes=[
            pltpu.VMEM((planes, height, across), BF16),
            pltpu.VMEM((1, NBIN), I32),
            pltpu.VMEM((4, NBIN), BF16),
            pltpu.VMEM((32, GROUPS * LANES), F32),
            pltpu.VMEM((planes + 2, height + 16, 2 * across), F32),
            pltpu.VMEM((2 * PHASES, 4, planes, block, across), F32),
            pltpu.VMEM((2, height, across), BF16),
            pltpu.VMEM((height, across), BF16),
            pltpu.VMEM((2, height, across), BF16),
            pltpu.VMEM((2, extended_rows, across), BF16),
            pltpu.VMEM((2, 3, extended_rows, across), BF16),
            pltpu.VMEM((2 * PHASES, 4, block, across), F32),
            pltpu.VMEM((PHASES, 3, 4, block, across), F32),
            pltpu.VMEM((PHASES, 2, nx, 5, block, across), I16),
            dma((3,)),
            dma((2,)), dma((2,)),
            dma((2,)), dma((2,)),
            dma((2, 3)), dma((2, 3)),
            dma((PHASES, 3)), dma((PHASES, 3)),
            dma((PHASES, nx)), dma((PHASES, nx)),
            dma((PHASES,)), dma((PHASES,)),
        ],
        compiler_params=pltpu.CompilerParams(collective_id=0, has_side_effects=True, vmem_limit_bytes=48 << 20),
    )(volume, hat_center.reshape(1, -1), tf_table)


def solution(mesh):
    in_specs = (P("gz", "gy", "gx"), P(), P())
    out_specs = P(None, "gy", None)
    return jax.shard_map(shards, mesh=mesh, in_specs=in_specs, out_specs=out_specs, check_vma=False)
```

time: 41.1 us -> 41.4 us (level)
  no operation moved by 1% of the time
where the time goes in v1:
time: 41.4 us; the launch traced here: 41.2 us
  Pallas kernels  37.8 us (91%)
  local copies, waits for them, and re-layouts  3.37 us (8%)
    pallas_call x1, Pallas kernels, shards(): pl.pallas_call(functools.partial(body, sizes), out_shape=jax.ShapeDtypeSt...  37.8 us
    unnamed x7, local copies, waits for them, and re-layouts  3.37 us

profile of v1, /device:TPU:0, one launch (start us, length us, event | category | flops | bytes accessed | tf_op | source)
XLA Modules:
  0.0 41.2 jit_solution(523022133670466977)
XLA Ops:
  0.0 0.0 copy-start.2
  0.0 0.7 %copy-done.2 = s32[256]{0:T(256)S(1)} copy-done((s32[256]{0:T(256)S(1)}, s32[256]{0:T(256)}, u32[]{:S(2)}) %copy-start.2) | copy-done | bytes 1048
  0.7 0.0 copy-start
  0.7 1.0 %copy-done = bf16[16,128,128]{2,1,0:T(8,128)(2,1)S(1)} copy-done((bf16[16,128,128]{2,1,0:T(8,128)(2,1)S(1)}, bf16[16,128,128]{2,1,0:T(8,128)(2,1)}, u32[]{:S(2)}) %copy-start) | copy-done | bytes 524312
  1.7 0.0 copy-start.1
  1.7 0.7 %copy-done.1 = bf16[4,256]{1,0:T(4,128)(2,1)S(1)} copy-done((bf16[4,256]{1,0:T(4,128)(2,1)S(1)}, bf16[4,256]{1,0:T(4,128)(2,1)}, u32[]{:S(2)}) %copy-start.1) | copy-done | bytes 2072
  2.4 37.8 %shard_map.37 = f32[4,128,512]{2,1,0:T(8,128)S(1)} custom-call(bf16[16,128,128]{2,1,0:T(8,128)(2,1)S(1)} %copy-done, s32[1,256]{1,0:T(1,128)S(1)} %bitcast.1, bf16[4,256]{1,0:T(4,128)(2,1)S(1)} %copy-done.1), custom_call_target="tpu_custom_call" | custom-call | tf_op jit(solution)/shard_map/pallas_call | solution.py:438
  40.2 1.0 %copy.5 = f32[4,128,512]{2,1,0:T(8,128)} copy(f32[4,128,512]{2,1,0:T(8,128)S(1)} %shard_map.37) | data formatting | bytes 2097152
Async XLA Ops:
  0.0 0.7 %copy-start.2 = (s32[256]{0:T(256)S(1)}, s32[256]{0:T(256)}, u32[]{:S(2)}) copy-start(s32[256]{0:T(256)} %param.4) | copy-start | bytes 3076
  0.7 1.0 %copy-start = (bf16[16,128,128]{2,1,0:T(8,128)(2,1)S(1)}, bf16[16,128,128]{2,1,0:T(8,128)(2,1)}, u32[]{:S(2)}) copy-start(bf16[16,128,128]{2,1,0:T(8,128)(2,1)} %vol_in.1) | copy-start | bytes 1572868
  1.7 0.7 %copy-start.1 = (bf16[4,256]{1,0:T(4,128)(2,1)S(1)}, bf16[4,256]{1,0:T(4,128)(2,1)}, u32[]{:S(2)}) copy-start(bf16[4,256]{1,0:T(4,128)(2,1)} %table_in.1) | copy-start | bytes 6148

commit v2 on v1

--- a/solution.py
+++ b/solution.py
@@ -17,7 +17,8 @@
 LANES = 128
 GROUPS = 7
 PHASES = 4
-AHEAD = 2
+BEFORE, MIDDLE, AFTER = 2, 1, 2
+AHEAD = BEFORE + MIDDLE + AFTER
 STEPS = 65534.0
 FINE = 64.0
 MESH = pl.DeviceIdType.MESH
@@ -113,7 +114,7 @@
     return (code[c].astype(I32).astype(F32) + 32767.0) * (jnp.exp2(power * (1.0 / FINE)) * (1.0 / STEPS))
 
 
-def body(sizes, vol_in, center_in, table_in, out, vol, center_ref, table_ref, tab, xsd, look, zhalo, face, faces, rows_out, rows_in, part, recv, code,
+def body(sizes, vol_in, center_in, table_in, out, vol, center_ref, table_ref, tab, xsd, look, zhalo, face, faces, rows_out, rows_in, part, pair, recv, code,
          ls, zs, zr, fs, fr, rs, rr, ps, pr, gs, gr, ns, nr):
     nx, ny, nz = sizes
     planes, height, across = vol.shape
@@ -179,17 +180,10 @@
         xsd[z + 1, pl.ds(8, height), :] = jnp.dot(cells, stencil, preferred_element_type=F32)
         return acc + edge_columns(cells, z + 1)
 
-    pl.semaphore_wait(barrier, count)
-
-    @pl.when(back)
-    def _():
-        to_back.start()
-
-    @pl.when(front)
-    def _():
-        to_front.start()
-
-    columns = lax.fori_loop(0, planes, own_plane, jnp.zeros((height, across), F32))
+    def own_planes(n, acc):
+        for k in range(4):
+            acc = own_plane(4 * n + k, acc)
+        return acc
 
     block = height // (2 * PHASES)
 
@@ -212,7 +206,23 @@
 
         lax.fori_loop(0, planes // 4, step, 0)
 
-    look_block(0)
+    for b in range(BEFORE):
+        look_block(b)
+
+    pl.semaphore_wait(barrier, count)
+
+    @pl.when(back)
+    def _():
+        to_back.start()
+
+    @pl.when(front)
+    def _():
+        to_front.start()
+
+    columns = lax.fori_loop(0, planes // 4, own_planes, jnp.zeros((height, across), F32))
+
+    for b in range(BEFORE, BEFORE + MIDDLE):
+        look_block(b)
 
     @pl.when(back)
     def _():
@@ -266,7 +276,7 @@
         def _(copy=copy):
             copy.start()
 
-    for b in range(1, AHEAD):
+    for b in range(BEFORE + MIDDLE, AHEAD):
         look_block(b)
 
     for sending, taking, copy in halo:
@@ -356,10 +366,7 @@
         return remote(part.at[2 * p], recv.at[p, 0], ps.at[p, 0], pr.at[p, 0], (ix, iy, near))
 
     def to_far(p):
-        return remote(part.at[2 * p + 1], recv.at[p, 1], ps.at[p, 1], pr.at[p, 1], (ix, iy, far))
-
-    def to_diag(p):
-        return remote(part.at[2 * p], recv.at[p, 2], ps.at[p, 2], pr.at[p, 2], (ix, iy, diag))
+        return remote(pair.at[p], recv.at[p, 1], ps.at[p, 1], pr.at[p, 1], (ix, iy, far))
 
     def along(p, t):
         tile = code.at[p, bit0, ix]
@@ -369,12 +376,16 @@
         half = code.at[p, bit0]
         return remote(half, half, ns.at[p], nr.at[p], (ix, iy, near))
 
+    def couple(p):
+        to_near(p).wait_recv()
+        mixed = fold([part[2 * p + 1, c] for c in range(4)], [recv[p, 0, c] for c in range(4)], bit0 == 0)
+        for c in range(4):
+            pair[p, c] = mixed[c]
+        to_far(p).start()
+
     def composite(p):
-        for copy in (to_near(p), to_diag(p), to_far(p)):
-            copy.wait_recv()
-        mine = fold([part[2 * p + 1, c] for c in range(4)], [recv[p, 0, c] for c in range(4)], bit0 == 0)
-        others = fold([recv[p, 1, c] for c in range(4)], [recv[p, 2, c] for c in range(4)], bit0 == 0)
-        quad = fold(mine, others, bit1 == 0)
+        to_far(p).wait_recv()
+        quad = fold([pair[p, c] for c in range(4)], [recv[p, 1, c] for c in range(4)], bit1 == 0)
         quad[3] = 1.0 - quad[3]
         encode(quad, code.at[p, bit0, ix])
         for t in range(nx - 1, 0, -1):
@@ -396,30 +407,28 @@
         remote(half, half, ns.at[p], nr.at[p], (ix, iy, near)).wait_recv()
         show(p, 1 - bit0)
 
+    def leave(p):
+        pass_on(p)
+        show(p, bit0)
+
+    last = PHASES - 1
     for b in range(2 * PHASES):
         render(b)
         p = b // 2
         if b % 2 == 0:
-            to_diag(p).start()
             to_near(p).start()
-            if p >= 1:
-                composite(p - 1)
         else:
-            to_far(p).start()
-            if p >= 2:
-                pass_on(p - 2)
-                show(p - 2, bit0)
-    last = PHASES - 1
-    for p in range(max(PHASES - 2, 0)):
-        take(p)
-    composite(last)
-    for p in range(max(PHASES - 2, 0), PHASES):
-        pass_on(p)
-        show(p, bit0)
-        take(p)
-
+            couple(p)
     for p in range(PHASES):
-        for copy in (to_near(p), to_diag(p), to_far(p), hand(p)):
+        composite(p)
+    leave(0)
+    for p in range(1, PHASES):
+        take(p - 1)
+        leave(p)
+    take(last)
+
+    for p in range(PHASES):
+        for copy in (to_near(p), to_far(p), hand(p)):
             copy.wait_send()
         for t in range(1, nx):
             along(p, t).wait_send()
@@ -453,13 +462,14 @@
             pltpu.VMEM((2, extended_rows, across), BF16),
             pltpu.VMEM((2, 3, extended_rows, across), BF16),
             pltpu.VMEM((2 * PHASES, 4, block, across), F32),
-            pltpu.VMEM((PHASES, 3, 4, block, across), F32),
+            pltpu.VMEM((PHASES, 4, block, across), F32),
+            pltpu.VMEM((PHASES, 2, 4, block, across), F32),
             pltpu.VMEM((PHASES, 2, nx, 5, block, across), I16),
             dma((3,)),
             dma((2,)), dma((2,)),
             dma((2,)), dma((2,)),
             dma((2, 3)), dma((2, 3)),
-            dma((PHASES, 3)), dma((PHASES, 3)),
+            dma((PHASES, 2)), dma((PHASES, 2)),
             dma((PHASES, nx)), dma((PHASES, nx)),
             dma((PHASES,)), dma((PHASES,)),
         ],

time: 41.4 us -> 37.4 us (0.903)
  Pallas kernels: 37.8 us -> 33.8 us
    pallas_call x1, Pallas kernels: 37.8 us -> 33.8 us  [shards(): pl.pallas_call(functools.partial(body, sizes), out_shape=jax.ShapeDtypeSt...]
where the time goes in v2:
time: 37.4 us; the launch traced here: 37.2 us
  Pallas kernels  33.8 us (90%)
  local copies, waits for them, and re-layouts  3.37 us (9%)
    pallas_call x1, Pallas kernels, shards(): pl.pallas_call(functools.partial(body, sizes), out_shape=jax.ShapeDtypeSt...  33.8 us
    unnamed x7, local copies, waits for them, and re-layouts  3.37 us

profile of v2, /device:TPU:0, one launch (start us, length us, event | category | flops | bytes accessed | tf_op | source)
XLA Modules:
  0.0 37.2 jit_solution(4410714417177081605)
XLA Ops:
  0.0 0.0 copy-start.2
  0.0 0.7 %copy-done.2 = s32[256]{0:T(256)S(1)} copy-done((s32[256]{0:T(256)S(1)}, s32[256]{0:T(256)}, u32[]{:S(2)}) %copy-start.2) | copy-done | bytes 1048
  0.7 0.0 copy-start
  0.7 1.0 %copy-done = bf16[16,128,128]{2,1,0:T(8,128)(2,1)S(1)} copy-done((bf16[16,128,128]{2,1,0:T(8,128)(2,1)S(1)}, bf16[16,128,128]{2,1,0:T(8,128)(2,1)}, u32[]{:S(2)}) %copy-start) | copy-done | bytes 524312
  1.7 0.0 copy-start.1
  1.7 0.7 %copy-done.1 = bf16[4,256]{1,0:T(4,128)(2,1)S(1)} copy-done((bf16[4,256]{1,0:T(4,128)(2,1)S(1)}, bf16[4,256]{1,0:T(4,128)(2,1)}, u32[]{:S(2)}) %copy-start.1) | copy-done | bytes 2072
  2.4 33.8 %shard_map.37 = f32[4,128,512]{2,1,0:T(8,128)S(1)} custom-call(bf16[16,128,128]{2,1,0:T(8,128)(2,1)S(1)} %copy-done, s32[1,256]{1,0:T(1,128)S(1)} %bitcast.1, bf16[4,256]{1,0:T(4,128)(2,1)S(1)} %copy-done.1), custom_call_target="tpu_custom_call" | custom-call | tf_op jit(solution)/shard_map/pallas_call | solution.py:447
  36.2 1.0 %copy.5 = f32[4,128,512]{2,1,0:T(8,128)} copy(f32[4,128,512]{2,1,0:T(8,128)S(1)} %shard_map.37) | data formatting | bytes 2097152
Async XLA Ops:
  0.0 0.7 %copy-start.2 = (s32[256]{0:T(256)S(1)}, s32[256]{0:T(256)}, u32[]{:S(2)}) copy-start(s32[256]{0:T(256)} %param.4) | copy-start | bytes 3076
  0.7 1.0 %copy-start = (bf16[16,128,128]{2,1,0:T(8,128)(2,1)S(1)}, bf16[16,128,128]{2,1,0:T(8,128)(2,1)}, u32[]{:S(2)}) copy-start(bf16[16,128,128]{2,1,0:T(8,128)(2,1)} %vol_in.1) | copy-start | bytes 1572868
  1.7 0.7 %copy-start.1 = (bf16[4,256]{1,0:T(4,128)(2,1)S(1)}, bf16[4,256]{1,0:T(4,128)(2,1)}, u32[]{:S(2)}) copy-start(bf16[4,256]{1,0:T(4,128)(2,1)} %table_in.1) | copy-start | bytes 6148

commit v3 on v2

--- a/solution.py
+++ b/solution.py
@@ -417,8 +417,9 @@
         p = b // 2
         if b % 2 == 0:
             to_near(p).start()
-        else:
-            couple(p)
+            if p >= 1:
+                couple(p - 1)
+    couple(last)
     for p in range(PHASES):
         composite(p)
     leave(0)
@@ -474,7 +475,7 @@
             dma((PHASES,)), dma((PHASES,)),
         ],
         compiler_params=pltpu.CompilerParams(collective_id=0, has_side_effects=True, vmem_limit_bytes=48 << 20),
-    )(volume, hat_center.reshape(1, -1), tf_table)
+    )(*(pltpu.with_memory_space_constraint(x, pltpu.MemorySpace.HBM) for x in (volume, hat_center.reshape(1, -1), tf_table)))
 
 
 def solution(mesh):

time: 37.4 us -> 35.1 us (0.939)
  local copies, waits for them, and re-layouts: 3.37 us -> 0.97 us
    unnamed x7 -> x1, local copies, waits for them, and re-layouts: 3.37 us -> 0.97 us
where the time goes in v3:
time: 35.1 us; the launch traced here: 34.9 us
  Pallas kernels  33.9 us (97%)
  local copies, waits for them, and re-layouts  0.97 us (3%)
    pallas_call x1, Pallas kernels, shards(): pl.pallas_call(functools.partial(body, sizes), out_shape=jax.ShapeDtypeSt...  33.9 us
    unnamed x1, local copies, waits for them, and re-layouts  0.97 us

profile of v3, /device:TPU:0, one launch (start us, length us, event | category | flops | bytes accessed | tf_op | source)
XLA Modules:
  0.0 34.9 jit_solution(2877089800849013480)
XLA Ops:
  0.0 33.9 %shard_map.37 = f32[4,128,512]{2,1,0:T(8,128)S(1)} custom-call(bf16[16,128,128]{2,1,0:T(8,128)(2,1)} %vol_in.1, s32[1,256]{1,0:T(1,128)} %bitcast.1, bf16[4,256]{1,0:T(4,128)(2,1)} %table_in.1), custom_call_target="tpu_custom_call" | custom-call | tf_op jit(solution)/shard_map/pallas_call | solution.py:448
  33.9 1.0 %copy.5 = f32[4,128,512]{2,1,0:T(8,128)} copy(f32[4,128,512]{2,1,0:T(8,128)S(1)} %shard_map.37) | data formatting | bytes 2097152

commit v4 on v3

--- a/solution.py
+++ b/solution.py
@@ -17,8 +17,8 @@
 LANES = 128
 GROUPS = 7
 PHASES = 4
-BEFORE, MIDDLE, AFTER = 2, 1, 2
-AHEAD = BEFORE + MIDDLE + AFTER
+BEFORE, AFTER = 1, 3
+AHEAD = BEFORE + AFTER
 STEPS = 65534.0
 FINE = 64.0
 MESH = pl.DeviceIdType.MESH
@@ -140,14 +140,20 @@
     for t in range(1, nx):
         pl.semaphore_signal(barrier, inc=1, device_id=((ix + t) % nx, iy, iz), device_id_type=MESH)
     count = 2 + nx
-    for s in (-1, 1):
-        for t in (-1, 0, 1):
-            there = (iy + s >= 0) & (iy + s < ny) & (ix + t >= 0) & (ix + t < nx)
-            count = count + there.astype(jnp.int32)
-
-            @pl.when(there)
-            def _(s=s, t=t):
-                pl.semaphore_signal(barrier, inc=1, device_id=(ix + t, iy + s, iz), device_id_type=MESH)
+
+    def inside(s, t, u):
+        x, y, z = ix + t, iy + s, iz + u
+        return (x >= 0) & (x < nx) & (y >= 0) & (y < ny) & (z >= 0) & (z < nz)
+
+    corners = [(0, t, u) for t in (-1, 1) for u in (-1, 1)]
+    corners += [(s, t, u) for s in (-1, 1) for t in (-1, 0, 1) for u in (-1, 0, 1)]
+    for s, t, u in corners:
+        there = inside(s, t, u)
+        count = count + there.astype(jnp.int32)
+
+        @pl.when(there)
+        def _(s=s, t=t, u=u):
+            pl.semaphore_signal(barrier, inc=1, device_id=(ix + t, iy + s, iz + u), device_id_type=MESH)
 
     def remote(src, dst, ssem, rsem, where):
         return pltpu.make_async_remote_copy(
@@ -185,6 +191,15 @@
             acc = own_plane(4 * n + k, acc)
         return acc
 
+    columns = lax.fori_loop(0, planes // 4, own_planes, jnp.zeros((height, across), F32))
+    face[...] = columns.astype(BF16)
+    count_rows = rows_out.shape[1]
+    for side, row in enumerate((0, height - 1)):
+        own = vol[:, row, :].astype(F32)
+        if count_rows > planes:
+            own = jnp.concatenate([own, jnp.zeros((count_rows - planes, across), F32)], axis=0)
+        rows_out[side] = own.astype(BF16)
+
     block = height // (2 * PHASES)
 
     def start_of(b):
@@ -211,28 +226,34 @@
 
     pl.semaphore_wait(barrier, count)
 
-    @pl.when(back)
-    def _():
-        to_back.start()
-
-    @pl.when(front)
-    def _():
-        to_front.start()
-
-    columns = lax.fori_loop(0, planes // 4, own_planes, jnp.zeros((height, across), F32))
-
-    for b in range(BEFORE, BEFORE + MIDDLE):
+    halo = [(back, front, to_back), (front, back, to_front)]
+    for u in (0, -1, 1):
+        for s, slot in ((1, 0), (-1, 1)):
+            copy = remote(face, faces.at[slot, 1 - u], fs.at[slot, 1 - u], fr.at[slot, 1 - u], (ix + s, iy, iz + u))
+            halo.append((inside(0, s, u), inside(0, -s, -u), copy))
+        for s, side in ((1, 0), (-1, 1)):
+            for t in (-1, 0, 1):
+                at = (side, 1 - t, 1 - u)
+                copy = remote(rows_out.at[1 - side], rows_in.at[at], rs.at[at], rr.at[at], (ix + t, iy + s, iz + u))
+                halo.append((inside(s, t, u), inside(-s, -t, -u), copy))
+    for sending, _, copy in halo:
+
+        @pl.when(sending)
+        def _(copy=copy):
+            copy.start()
+
+    for b in range(BEFORE, AHEAD):
         look_block(b)
 
-    @pl.when(back)
-    def _():
-        to_back.wait_send()
-        to_front.wait_recv()
-
-    @pl.when(front)
-    def _():
-        to_front.wait_send()
-        to_back.wait_recv()
+    for sending, taking, copy in halo:
+
+        @pl.when(taking)
+        def _(copy=copy):
+            copy.wait_recv()
+
+        @pl.when(sending)
+        def _(copy=copy):
+            copy.wait_send()
 
     @pl.when(jnp.logical_not(front))
     def _():
@@ -243,75 +264,39 @@
         zhalo[1] = jnp.zeros_like(zhalo[1])
 
     for slot, plane in ((0, 0), (1, planes + 1)):
-        cells = zhalo[slot]
-        xsd[plane, pl.ds(8, height), :] = jnp.dot(cells, stencil, preferred_element_type=F32)
-        columns = columns + edge_columns(cells, plane)
-    face[...] = columns.astype(BF16)
-
-    def edge_rows(row):
-        own = vol[:, row, :].astype(F32)
-        pad = jnp.zeros((rows_out.shape[1] - planes - 2, across), F32)
-        ends = [zhalo[slot, row : row + 1, :].astype(F32) for slot in (0, 1)]
-        return jnp.concatenate([ends[0], own, ends[1], pad], axis=0).astype(BF16)
-
-    rows_out[0] = edge_rows(0)
-    rows_out[1] = edge_rows(height - 1)
-
-    halo = []
-    for s, slot in ((1, 0), (-1, 1)):
-        sending = (ix + s >= 0) & (ix + s < nx)
-        taking = (ix - s >= 0) & (ix - s < nx)
-        halo.append((sending, taking, remote(face, faces.at[slot], fs.at[slot], fr.at[slot], (ix + s, iy, iz))))
-    for s, side in ((1, 0), (-1, 1)):
-        for t in (-1, 0, 1):
-            slot = 1 - t
-            sending = (iy + s >= 0) & (iy + s < ny) & (ix + t >= 0) & (ix + t < nx)
-            taking = (iy - s >= 0) & (iy - s < ny) & (ix - t >= 0) & (ix - t < nx)
-            halo.append(
-                (sending, taking, remote(rows_out.at[1 - side], rows_in.at[side, slot], rs.at[side, slot], rr.at[side, slot], (ix + t, iy + s, iz)))
-            )
-    for sending, _, copy in halo:
-
-        @pl.when(sending)
-        def _(copy=copy):
-            copy.start()
-
-    for b in range(BEFORE + MIDDLE, AHEAD):
-        look_block(b)
-
-    for sending, taking, copy in halo:
-
-        @pl.when(taking)
-        def _(copy=copy):
-            copy.wait_recv()
-
-        @pl.when(sending)
-        def _(copy=copy):
-            copy.wait_send()
+        xsd[plane, pl.ds(8, height), :] = jnp.dot(zhalo[slot], stencil, preferred_element_type=F32)
 
     lane = lax.broadcasted_iota(jnp.int32, (height, across), 1)
-    both = jnp.where(lane % 2 == 1, faces[0].astype(F32), faces[1].astype(F32))
+
+    def both_sides(u):
+        return jnp.where(lane % 2 == 1, faces[0, u].astype(F32), faces[1, u].astype(F32))
+
+    both = both_sides(1)
     ends = jnp.where((lane == 0) | (lane == across - 1), 1.0, 0.0)
     sign = jnp.where(lane == 0, -1.0, jnp.where(lane == across - 1, 1.0, 0.0))
 
+    def place(z, sides, plane):
+        placed = pltpu.roll(sides, across - 2 * plane - 1, 1)
+        xsd[z, pl.ds(8, height), :] += jnp.concatenate([placed * ends, placed * sign], axis=1)
+
     def add_columns(z, carry):
-        placed = pltpu.roll(both, across - 2 * z - 1, 1)
-        xsd[z, pl.ds(8, height), :] += jnp.concatenate([placed * ends, placed * sign], axis=1)
+        place(z, both, z)
         return carry
 
-    lax.fori_loop(0, planes + 2, add_columns, 0)
-    count_rows = rows_out.shape[1]
+    lax.fori_loop(1, planes + 1, add_columns, 0)
+    place(0, both_sides(0), planes)
+    place(planes + 1, both_sides(2), 1)
+    short = lax.broadcasted_iota(jnp.int32, (count_rows, across), 1)
     for side in (0, 1):
-        strip = jnp.dot(rows_in[side, 1], stencil, preferred_element_type=F32)
-        left = pltpu.roll(rows_in[side, 0].astype(F32), 1, 1)
-        right = pltpu.roll(rows_in[side, 2].astype(F32), across - 1, 1)
-        short = lax.broadcasted_iota(jnp.int32, (count_rows, across), 1)
-        left = jnp.where(short == 0, left, 0.0)
-        right = jnp.where(short == across - 1, right, 0.0)
-        strip = strip + jnp.concatenate([left + right, right - left], axis=1)
         row = 7 if side == 0 else 8 + height
-        for z in range(planes + 2):
-            xsd[z, row : row + 1, :] = strip[z : z + 1]
+        for u in range(3):
+            strip = jnp.dot(rows_in[side, 1, u], stencil, preferred_element_type=F32)
+            left = jnp.where(short == 0, pltpu.roll(rows_in[side, 0, u].astype(F32), 1, 1), 0.0)
+            right = jnp.where(short == across - 1, pltpu.roll(rows_in[side, 2, u].astype(F32), across - 1, 1), 0.0)
+            strip = strip + jnp.concatenate([left + right, right - left], axis=1)
+            for z in range(planes) if u == 1 else ((planes - 1,) if u == 0 else (0,)):
+                to = z + 1 if u == 1 else (0 if u == 0 else planes + 1)
+                xsd[to, row : row + 1, :] = strip[z : z + 1]
 
     shade_scale = (1.0 - ambient) / (32.0 * 3.0**0.5)
 
@@ -440,7 +425,7 @@
     sizes = tuple(lax.axis_size(a) for a in ("gx", "gy", "gz"))
     nx = sizes[0]
     assert sizes[2] == 4 and across == LANES and height % (32 * PHASES) == 0
-    extended_rows = -(-(planes + 2) // 16) * 16
+    padded = -(-planes // 16) * 16
     block = height // (2 * PHASES)
     dma = pltpu.SemaphoreType.DMA
     vmem = pl.BlockSpec(memory_space=pltpu.VMEM)
@@ -459,17 +444,17 @@
             pltpu.VMEM((2 * PHASES, 4, planes, block, across), F32),
             pltpu.VMEM((2, height, across), BF16),
             pltpu.VMEM((height, across), BF16),
-            pltpu.VMEM((2, height, across), BF16),
-            pltpu.VMEM((2, extended_rows, across), BF16),
-            pltpu.VMEM((2, 3, extended_rows, across), BF16),
+            pltpu.VMEM((2, 3, height, across), BF16),
+            pltpu.VMEM((2, padded, across), BF16),
+            pltpu.VMEM((2, 3, 3, padded, across), BF16),
             pltpu.VMEM((2 * PHASES, 4, block, across), F32),
             pltpu.VMEM((PHASES, 4, block, across), F32),
             pltpu.VMEM((PHASES, 2, 4, block, across), F32),
             pltpu.VMEM((PHASES, 2, nx, 5, block, across), I16),
             dma((3,)),
             dma((2,)), dma((2,)),
-            dma((2,)), dma((2,)),
             dma((2, 3)), dma((2, 3)),
+            dma((2, 3, 3)), dma((2, 3, 3)),
             dma((PHASES, 2)), dma((PHASES, 2)),
             dma((PHASES, nx)), dma((PHASES, nx)),
             dma((PHASES,)), dma((PHASES,)),

time: 35.1 us -> 32.9 us (0.937)
  Pallas kernels: 33.9 us -> 31.8 us
    pallas_call x1, Pallas kernels: 33.9 us -> 31.8 us  [shards(): pl.pallas_call(functools.partial(body, sizes), out_shape=jax.ShapeDtypeSt...]
where the time goes in v4:
time: 32.9 us; the launch traced here: 32.8 us
  Pallas kernels  31.8 us (97%)
  local copies, waits for them, and re-layouts  0.97 us (3%)
    pallas_call x1, Pallas kernels, shards(): pl.pallas_call(functools.partial(body, sizes), out_shape=jax.ShapeDtypeSt...  31.8 us
    unnamed x1, local copies, waits for them, and re-layouts  0.97 us

profile of v4, /device:TPU:0, one launch (start us, length us, event | category | flops | bytes accessed | tf_op | source)
XLA Modules:
  0.0 32.8 jit_solution(17311400473511246831)
XLA Ops:
  0.0 31.8 %shard_map.37 = f32[4,128,512]{2,1,0:T(8,128)S(1)} custom-call(bf16[16,128,128]{2,1,0:T(8,128)(2,1)} %vol_in.1, s32[1,256]{1,0:T(1,128)} %bitcast.1, bf16[4,256]{1,0:T(4,128)(2,1)} %table_in.1), custom_call_target="tpu_custom_call" | custom-call | tf_op jit(solution)/shard_map/pallas_call | solution.py:433
  31.8 1.0 %copy.5 = f32[4,128,512]{2,1,0:T(8,128)} copy(f32[4,128,512]{2,1,0:T(8,128)S(1)} %shard_map.37) | data formatting | bytes 2097152
